TPU v7x, 512 devices: a whole 4x4x16 slice. The times are simulated.
512 devices in a mesh: row: 16 (over z), col: 32 (over y, x, core).
Axes of the slice: x: 4, y: 4, z: 16, core: 2. Of those that a mesh axis runs over, the one named last changes fastest.
Arguments:
- new_keys: bfloat16 [1024, 28672], P('col', 'row'), may hold values from -6 to 6
- precision: bfloat16 [28672, 28672], P('row', 'col'), may hold values from -0.03125 to 0.03125
- stored_keys: bfloat16 [32, 256, 28672], P('row', None, 'col'), may hold values from -0.03125 to 0.03125
- pair_batch: int32 [16, 24], replicated, may hold values from 0 to 31, as said below
- pair_count: int32 [16], replicated, may hold values from 8 to 24, as said below
- batch_length: int32 [32], replicated, may hold values from 64 to 256
- batch_slot: int32 [32], replicated, may hold values from 0 to 31, each once
Outputs:
- whitened: bfloat16 [1024, 28672], P('row', 'col')
- intersections: float32 [16, 24, 64, 256], P('row', None, 'col')
Inputs may be any that keep to these rules, and one draw needn't show every extreme that they name: `pair_batch`: the ids in one block's row are distinct; ids at places at or beyond the block's count are ignored. `pair_count`: some block lists exactly 24 batches. `batch_slot`: every store slot belongs to exactly one batch.
All inputs are finite; a program needn't handle non-finite values.
Results may differ from a plain program's by a relative error of at most 0.0029.
Values may be sent and summed in bfloat16 or wider, within the bound.
A program may use at most 64 MiB of HBM per device.

v0:
```python
import jax
import jax.numpy as jnp
from jax import lax
from jax.sharding import PartitionSpec as P


def shards(new_keys, precision, stored_keys, pair_batch, pair_count, batch_length, batch_slot):
    row_count = lax.axis_size("row")
    col_count = lax.axis_size("col")
    row_index = lax.axis_index("row")
    total_keys = new_keys.shape[0] * col_count
    block_keys = total_keys // row_count
    part_keys = block_keys // col_count
    local_batches, batch_keys, width = stored_keys.shape
    partial_value = jnp.dot(
        lax.all_gather(new_keys, "col", axis=0, tiled=True),
        precision,
        preferred_element_type=jnp.float32,
    )
    summed = lax.psum_scatter(partial_value, "row", scatter_dimension=0, tiled=True)
    whitened = summed.astype(jnp.bfloat16)
    every_row = lax.all_gather(whitened, "row", axis=0, tiled=True)
    rows = every_row.reshape(row_count, col_count, part_keys, width)
    terms = jnp.einsum("bcid,sjd->csbij", rows, stored_keys, preferred_element_type=jnp.float32)
    mine = lax.psum_scatter(terms, "col", scatter_dimension=0, tiled=True)[0]
    routed = lax.all_to_all(mine, "row", split_axis=1, concat_axis=0, tiled=True)
    table = routed[:, 0]
    listed = pair_batch[row_index]
    slots = batch_slot[listed]
    lengths = batch_length[listed]
    count = pair_count[row_index]
    picked = jnp.take(table, slots, axis=0)
    places = jnp.arange(slots.shape[0], dtype=jnp.int32)
    columns = jnp.arange(batch_keys, dtype=jnp.int32)
    keep = (places < count)[:, None, None] & (columns[None, None, :] < lengths[:, None, None])
    shares = jnp.where(keep, picked, jnp.zeros_like(picked))
    return (whitened, shares[None])


def solution(mesh):
    placed = (P("col", "row"), P("row", "col"), P("row", None, "col"), P(), P(), P(), P())
    return jax.shard_map(
        shards,
        mesh=mesh,
        in_specs=placed,
        out_specs=(P("row", "col"), P("row", None, "col", None)),
        check_vma=False,
    )
```

profile of v0, /device:TPU:6, one launch (start us, length us, event | category | flops | bytes accessed | tf_op | source)
XLA Modules:
  0.0 379.6 jit_solution(4652722605744629083)
XLA Ops:
  7.2 0.0 copy-start
  7.2 0.0 all-gather.3.cloned.1.call-start
  7.2 0.7 all-gather.3.cloned.1.call-update
  7.9 0.0 reduce-scatter.3.cloned.1.call-start
  8.0 68.1 %all-gather.3.cloned.1.call-done = bf16[1024,1792]{1,0:T(8,128)(2,1)} async-done(((bf16[32,1792]{1,0:T(8,128)(2,1)}), bf16[1024,1792]{1,0:T(8,128)(2,1)}) %all-gather.3.cloned.1.call-update) | async-done | bytes 3670032 | tf_op jit(solution)/shard_map/all_gather | solution.py:16
  76.0 0.0 copy-done
  76.0 7.8 %fusion.10 = f32[1024,896]{1,0:T(8,128)} fusion(bf16[1024,1792]{1,0:T(8,128)(2,1)} %all-gather.3.cloned.1.call-done, bf16[1792,896]{1,0:T(8,128)(2,1)S(1)} %copy-done), kind=kOutput, calls=%fused_computation.20 | convolution fusion | flops 3288334336 | bytes 10551296 | tf_op jit(solution)/shard_map/dot_general | solution.py:15
  83.8 0.0 reduce-scatter.3.cloned.1.call-update
  83.8 0.0 all-gather.5.cloned.1.call-start
  83.9 78.2 %reduce-scatter.3.cloned.1.call-done = f32[64,896]{1,0:T(8,128)} async-done(((f32[1024,896]{1,0:T(8,128)}), f32[64,896]{1,0:T(8,128)}) %reduce-scatter.3.cloned.1.call-update) | async-done | bytes 229392 | tf_op jit(solution)/shard_map/reduce_scatter | solution.py:20
  162.1 1.6 convert_element_type.3
  163.7 0.0 all-gather.5.cloned.1.call-update
  163.7 0.0 reduce-scatter.5.cloned.1.call-start
  163.8 72.0 %all-gather.5.cloned.1.call-done = bf16[1024,896]{1,0:T(8,128)(2,1)} async-done(((bf16[64,896]{1,0:T(8,128)(2,1)}), bf16[1024,896]{1,0:T(8,128)(2,1)}) %all-gather.5.cloned.1.call-update) | async-done | bytes 1835024 | tf_op jit(solution)/shard_map/all_gather | solution.py:22
  235.8 4.8 %reshape.105 = bf16[16,32,2,896]{3,2,1,0:T(2,128)(2,1)} reshape(bf16[1024,896]{1,0:T(8,128)(2,1)} %all-gather.5.cloned.1.call-done) | data formatting | bytes 3670016 | tf_op jit(solution)/shard_map/reshape | solution.py:23
  240.7 3.0 fusion.2
  243.7 0.0 copy-start.3
  243.7 0.0 copy-start.1
  243.7 0.0 copy-start.2
  243.7 2.5 copy.16
  246.2 0.0 reduce-scatter.5.cloned.1.call-update
  246.3 0.0 copy-done.3
  246.3 0.6 dynamic_slice.6
  246.9 0.7 fusion.8
  247.6 0.0 copy-done.1
  247.6 0.7 gather_fusion.1
  248.3 96.7 %reduce-scatter.5.cloned.1.call-done = f32[1,2,16,2,256]{4,2,3,1,0:T(8,128)} async-done(((f32[32,2,16,2,256]{4,2,3,1,0:T(8,128)}), f32[1,2,16,2,256]{4,2,3,1,0:T(8,128)}) %reduce-scatter.5.cloned.1.call-update) | async-done | bytes 65552 | tf_op jit(solution)/shard_map/reduce_scatter | solution.py:25
  345.1 1.5 copy.17
  346.6 12.3 %all-to-all-start = ((f32[2,16,2,256]{3,2,0,1:T(2,128)}), f32[2,16,2,256]{3,2,0,1:T(2,128)S(1)}, u32[]{:S(2)}, u32[]{:S(2)}) async-start(f32[2,16,2,256]{3,2,0,1:T(2,128)} %copy.17), calls=%async_computation.2 | async-start | bytes 131072 | tf_op jit(solution)/shard_map/all_to_all | solution.py:26
  358.9 0.7 iota_compare_fusion.1
  359.6 0.0 copy-done.2
  359.6 0.7 gather_fusion
  360.3 0.1 fusion.7
  360.4 11.4 %all-to-all-done = f32[2,16,2,256]{3,2,0,1:T(2,128)S(1)} async-done(((f32[2,16,2,256]{3,2,0,1:T(2,128)}), f32[2,16,2,256]{3,2,0,1:T(2,128)S(1)}, u32[]{:S(2)}, u32[]{:S(2)}) %all-to-all-start) | async-done | bytes 65568 | tf_op jit(solution)/shard_map/all_to_all | solution.py:26
  371.8 0.6 gather_fusion.2
  372.4 0.7 fusion.6
  (4 shorter events, 0.0 us)
Async XLA Ops:
  7.2 68.9 %copy-start = (bf16[1792,896]{1,0:T(8,128)(2,1)S(1)}, bf16[1792,896]{1,0:T(8,128)(2,1)}, u32[]{:S(2)}) copy-start(bf16[1792,896]{1,0:T(8,128)(2,1)} %param.8) | copy-start | bytes 9633796
  7.2 68.9 %all-gather.3.cloned.1.call-start = ((), (), s32[]{:S(2)}) async-start(), calls=%async_computation.3 | async-start | bytes 3784704 | tf_op jit(solution)/shard_map/all_gather | solution.py:16
  7.9 154.2 %reduce-scatter.3.cloned.1.call-start = ((), (), s32[]{:S(2)}) async-start(), calls=%async_computation.4 | async-start | bytes 3899392 | tf_op jit(solution)/shard_map/reduce_scatter | solution.py:20
  83.8 152.0 %all-gather.5.cloned.1.call-start = ((), (), s32[]{:S(2)}) async-start(), calls=%async_computation.5 | async-start | bytes 1949696 | tf_op jit(solution)/shard_map/all_gather | solution.py:22
  163.7 181.3 %reduce-scatter.5.cloned.1.call-start = ((), (), s32[]{:S(2)}) async-start(), calls=%async_computation.6 | async-start | bytes 2162688 | tf_op jit(solution)/shard_map/reduce_scatter | solution.py:25
  243.7 2.6 copy-start.3
  243.7 3.9 %copy-start.1 = (s32[32]{0:T(128)S(1)}, s32[32]{0:T(128)}, u32[]{:S(2)}) copy-start(s32[32]{0:T(128)} %param.13) | copy-start | bytes 388
  243.7 115.9 %copy-start.2 = (s32[32]{0:T(128)S(1)}, s32[32]{0:T(128)}, u32[]{:S(2)}) copy-start(s32[32]{0:T(128)} %param.12) | copy-start | bytes 388
  346.6 25.2 %all-to-all-start = ((f32[2,16,2,256]{3,2,0,1:T(2,128)}), f32[2,16,2,256]{3,2,0,1:T(2,128)S(1)}, u32[]{:S(2)}, u32[]{:S(2)}) async-start(f32[2,16,2,256]{3,2,0,1:T(2,128)} %copy.17), calls=%async_computation.2 | async-start | bytes 131072 | tf_op jit(solution)/shard_map/all_to_all | solution.py:26
Sparse Core Ops, SparseCore 0:
  11.1 64.8 all-gather.2
  84.0 78.1 reduce-scatter.2
  164.8 71.0 all-gather.4
  246.4 98.6 reduce-scatter.4
where the time goes:
time: 380 us
  waiting for transfers between devices  327 us (86%)
  between operations  13.9 us (4%)
  starting transfers between devices  12.5 us (3%)
  local copies, waits for them, and re-layouts  11.5 us (3%)
  matrix products  10.8 us (3%)
    reduce_scatter x1, waiting for transfers between devices, shards(): mine = lax.psum_scatter(terms, 'col', scatter_dimension=0, tiled=True)[0]  96.7 us
    reduce_scatter x1, waiting for transfers between devices, shards(): lax.psum_scatter(partial_value, 'row', scatter_dimension=0, tiled=True)  78.2 us
    all_gather x1, waiting for transfers between devices, shards(): every_row = lax.all_gather(whitened, 'row', axis=0, tiled=True)  72 us
    all_gather x1, waiting for transfers between devices, shards(): lax.all_gather(new_keys, 'col', axis=0, tiled=True)  68.1 us
    all_to_all x1, starting transfers between devices, shards(): lax.all_to_all(mine, 'row', split_axis=1, concat_axis=0, tiled=True)  12.3 us
    all_to_all x1, waiting for transfers between devices, shards(): lax.all_to_all(mine, 'row', split_axis=1, concat_axis=0, tiled=True)  11.4 us
    dot_general x1, matrix products, shards(): jnp.dot(lax.all_gather(new_keys, 'col', axis=0, tiled=True), precision, p...  7.77 us
  transfers between devices with their start and end apart: 5, of which 5 were waited for; matrix products, arithmetic and copies ran while one was open for 1% of the time, Pallas kernels for 0%

commit v1 on v0

--- a/solution.py
+++ b/solution.py
@@ -2,6 +2,35 @@
 import jax.numpy as jnp
 from jax import lax
 from jax.sharding import PartitionSpec as P
+
+
+def assign_node(local_block, row_dim, block_here):
+    seen_now = local_block.shape
+    everything = local_block.reshape(
+        *seen_now[:row_dim], block_here, seen_now[row_dim] // block_here, *seen_now[row_dim + 1 :]
+    )
+    passed = jnp.moveaxis(everything, row_dim, 0)
+    return passed
+
+
+def cover_the_unit(inner_x, ndim_at):
+    arr_next = list(inner_x.shape[1:])
+    arr_next[ndim_at] *= inner_x.shape[0]
+    local_part = jnp.moveaxis(inner_x, 0, ndim_at).reshape(arr_next)
+    return local_part
+
+
+def supply_the_paths(field, axis_tag, local_x, panel):
+    r_now, a_next = (lax.axis_size(axis_tag), lax.axis_index(axis_tag))
+    main = assign_node(field, local_x, r_now)
+    block_list = [main[a_next]]
+    for no in range(1, r_now):
+        y1 = main[a_next ^ no]
+        block_list.append(lax.ppermute(y1, axis_tag, [(jj, jj ^ no) for jj in range(r_now)]))
+    tmp = jnp.stack(block_list, 0)
+    main = tmp[a_next ^ jnp.arange(r_now)]
+    opened = cover_the_unit(main, panel)
+    return opened
 
 
 def shards(new_keys, precision, stored_keys, pair_batch, pair_count, batch_length, batch_slot):
@@ -23,7 +52,7 @@
     rows = every_row.reshape(row_count, col_count, part_keys, width)
     terms = jnp.einsum("bcid,sjd->csbij", rows, stored_keys, preferred_element_type=jnp.float32)
     mine = lax.psum_scatter(terms, "col", scatter_dimension=0, tiled=True)[0]
-    routed = lax.all_to_all(mine, "row", split_axis=1, concat_axis=0, tiled=True)
+    routed = supply_the_paths(mine, "row", 1, 0)
     table = routed[:, 0]
     listed = pair_batch[row_index]
     slots = batch_slot[listed]

time: 380 us -> 440 us (1.16)
  starting transfers between devices: 12.5 us -> 76.5 us
  waiting for transfers between devices: 327 us -> 319 us
    ppermute x0 -> x15, starting transfers between devices: none -> 76.4 us  [supply_the_paths(): lax.ppermute(y1, axis_tag, [(jj, jj ^ no) for jj in range(r_now)])]
    all_to_all x1 -> x0, starting transfers between devices: 12.3 us -> none  [shards(): lax.all_to_all(mine, 'row', split_axis=1, concat_axis=0, tiled=True)]
    all_to_all x1 -> x0, waiting for transfers between devices: 11.4 us -> none  [shards(): lax.all_to_all(mine, 'row', split_axis=1, concat_axis=0, tiled=True)]
    ppermute x0 -> x15, waiting for transfers between devices: none -> 4.72 us  [supply_the_paths(): lax.ppermute(y1, axis_tag, [(jj, jj ^ no) for jj in range(r_now)])]
  transfers between devices with their start and end apart: 5 -> 19, of which waited for: 5 -> 5; matrix products, arithmetic and copies ran while one was open for 1% -> 1% of each run, Pallas kernels for 0% -> 0%
where the time goes in v1:
time: 440 us; the launch traced here: 437 us
  waiting for transfers between devices  319 us (72%)
  starting transfers between devices  76.5 us (17%)
  between operations  14.3 us (3%)
  local copies, waits for them, and re-layouts  12.4 us (3%)
  matrix products  10.8 us (2%)
    reduce_scatter x1, waiting for transfers between devices, shards(): mine = lax.psum_scatter(terms, 'col', scatter_dimension=0, tiled=True)[0]  95.2 us
    reduce_scatter x1, waiting for transfers between devices, shards(): lax.psum_scatter(partial_value, 'row', scatter_dimension=0, tiled=True)  78.2 us
    ppermute x15, starting transfers between devices, supply_the_paths(): lax.ppermute(y1, axis_tag, [(jj, jj ^ no) for jj in range(r_now)])  76.4 us
    all_gather x1, waiting for transfers between devices, shards(): every_row = lax.all_gather(whitened, 'row', axis=0, tiled=True)  72 us
    all_gather x1, waiting for transfers between devices, shards(): lax.all_gather(new_keys, 'col', axis=0, tiled=True)  68.1 us
  transfers between devices with their start and end apart: 19, of which 5 were waited for; matrix products, arithmetic and copies ran while one was open for 1% of the time, Pallas kernels for 0%

profile of v1, /device:TPU:6, one launch (start us, length us, event | category | flops | bytes accessed | tf_op | source)
XLA Modules:
  0.0 436.8 jit_solution(4665073949928509452)
XLA Ops:
  7.2 0.0 copy-start
  7.2 0.0 all-gather.3.cloned.1.call-start
  7.2 0.7 all-gather.3.cloned.1.call-update
  7.9 0.0 reduce-scatter.3.cloned.1.call-start
  8.0 68.1 %all-gather.3.cloned.1.call-done = bf16[1024,1792]{1,0:T(8,128)(2,1)} async-done(((bf16[32,1792]{1,0:T(8,128)(2,1)}), bf16[1024,1792]{1,0:T(8,128)(2,1)}) %all-gather.3.cloned.1.call-update) | async-done | bytes 3670032 | tf_op jit(solution)/shard_map/all_gather | solution.py:45
  76.0 7.8 %fusion.12 = f32[1024,896]{1,0:T(8,128)} fusion(bf16[1024,1792]{1,0:T(8,128)(2,1)} %all-gather.3.cloned.1.call-done, bf16[1792,896]{1,0:T(8,128)(2,1)S(1)} %copy-done), kind=kOutput, calls=%fused_computation.73 | convolution fusion | flops 3288334336 | bytes 10551296 | tf_op jit(solution)/shard_map/dot_general | solution.py:44
  83.8 0.0 reduce-scatter.3.cloned.1.call-update
  83.8 0.0 all-gather.5.cloned.1.call-start
  83.9 78.2 %reduce-scatter.3.cloned.1.call-done = f32[64,896]{1,0:T(8,128)} async-done(((f32[1024,896]{1,0:T(8,128)}), f32[64,896]{1,0:T(8,128)}) %reduce-scatter.3.cloned.1.call-update) | async-done | bytes 229392 | tf_op jit(solution)/shard_map/reduce_scatter | solution.py:49
  162.1 1.6 convert_element_type.3
  163.7 0.0 all-gather.5.cloned.1.call-update
  163.7 0.0 reduce-scatter.5.cloned.1.call-start
  163.8 72.0 %all-gather.5.cloned.1.call-done = bf16[1024,896]{1,0:T(8,128)(2,1)} async-done(((bf16[64,896]{1,0:T(8,128)(2,1)}), bf16[1024,896]{1,0:T(8,128)(2,1)}) %all-gather.5.cloned.1.call-update) | async-done | bytes 1835024 | tf_op jit(solution)/shard_map/all_gather | solution.py:51
  235.8 4.8 %reshape.183 = bf16[16,32,2,896]{3,2,1,0:T(2,128)(2,1)} reshape(bf16[1024,896]{1,0:T(8,128)(2,1)} %all-gather.5.cloned.1.call-done) | data formatting | bytes 3670016 | tf_op jit(solution)/shard_map/reshape | solution.py:52
  240.6 3.0 fusion.2
  243.7 0.0 copy-start.1
  243.7 0.0 copy-start.2
  243.7 0.0 copy-start.3
  243.7 2.5 copy.13
  246.2 0.0 reduce-scatter.5.cloned.1.call-update
  246.3 0.7 fusion.8
  247.0 0.7 gather_fusion.1
  247.7 0.7 gather_fusion
  248.4 0.6 dynamic_slice.6
  249.0 0.6 iota_compare_fusion.1
  249.8 0.1 fusion.7
  249.8 95.2 %reduce-scatter.5.cloned.1.call-done = f32[1,2,16,2,256]{4,2,3,1,0:T(8,128)} async-done(((f32[32,2,16,2,256]{4,2,3,1,0:T(8,128)}), f32[1,2,16,2,256]{4,2,3,1,0:T(8,128)}) %reduce-scatter.5.cloned.1.call-update) | async-done | bytes 65552 | tf_op jit(solution)/shard_map/reduce_scatter | solution.py:54
  345.1 1.6 constant_dynamic-slice_fusion
  346.6 3.5 collective-permute-start
  350.1 4.5 %collective-permute-start.1 = (f32[2,1,2,256]{3,2,0,1:T(2,128)S(1)}, f32[2,1,2,256]{3,2,0,1:T(2,128)S(1)}, u32[]{:S(2)}, u32[]{:S(2)}) collective-permute-start(f32[2,1,2,256]{3,2,0,1:T(2,128)S(1)} %bitcast.120), channel_id=1, source_target_pairs={{0,64},{32,96},{64,0},{96,32},{128,192},{160,224},{192,128},{224,1... | collective-permute-start | bytes 12296 | tf_op jit(solution)/shard_map/ppermute | solution.py:29
  354.6 2.2 collective-permute-start.2
  356.8 7.7 %collective-permute-start.3 = (f32[2,1,2,256]{3,2,0,1:T(2,128)S(1)}, f32[2,1,2,256]{3,2,0,1:T(2,128)S(1)}, u32[]{:S(2)}, u32[]{:S(2)}) collective-permute-start(f32[2,1,2,256]{3,2,0,1:T(2,128)S(1)} %bitcast.118), channel_id=1, source_target_pairs={{0,128},{32,160},{64,192},{96,224},{128,0},{160,32},{192,64},{224,... | collective-permute-start | bytes 12296 | tf_op jit(solution)/shard_map/ppermute | solution.py:29
  364.5 2.2 collective-permute-start.4
  366.8 9.7 %collective-permute-start.5 = (f32[2,1,2,256]{3,2,0,1:T(2,128)S(1)}, f32[2,1,2,256]{3,2,0,1:T(2,128)S(1)}, u32[]{:S(2)}, u32[]{:S(2)}) collective-permute-start(f32[2,1,2,256]{3,2,0,1:T(2,128)S(1)} %bitcast.116), channel_id=1, source_target_pairs={{0,192},{32,224},{64,128},{96,160},{128,64},{160,96},{192,0},{224,... | collective-permute-start | bytes 12296 | tf_op jit(solution)/shard_map/ppermute | solution.py:29
  376.5 0.0 collective-permute-done.1
  376.5 1.9 collective-permute-start.6
  378.5 12.7 %collective-permute-start.7 = (f32[2,1,2,256]{3,2,0,1:T(2,128)S(1)}, f32[2,1,2,256]{3,2,0,1:T(2,128)S(1)}, u32[]{:S(2)}, u32[]{:S(2)}) collective-permute-start(f32[2,1,2,256]{3,2,0,1:T(2,128)S(1)} %bitcast.114), channel_id=1, source_target_pairs={{0,256},{32,288},{64,320},{96,352},{128,384},{160,416},{192,448},{... | collective-permute-start | bytes 12296 | tf_op jit(solution)/shard_map/ppermute | solution.py:29
  391.2 1.9 collective-permute-start.8
  393.1 6.6 %collective-permute-start.9 = (f32[2,1,2,256]{3,2,0,1:T(2,128)S(1)}, f32[2,1,2,256]{3,2,0,1:T(2,128)S(1)}, u32[]{:S(2)}, u32[]{:S(2)}) collective-permute-start(f32[2,1,2,256]{3,2,0,1:T(2,128)S(1)} %bitcast.112), channel_id=1, source_target_pairs={{0,320},{32,352},{64,256},{96,288},{128,448},{160,480},{192,384},{... | collective-permute-start | bytes 12296 | tf_op jit(solution)/shard_map/ppermute | solution.py:29
  399.8 5.2 %collective-permute-start.10 = (f32[2,1,2,256]{3,2,0,1:T(2,128)S(1)}, f32[2,1,2,256]{3,2,0,1:T(2,128)S(1)}, u32[]{:S(2)}, u32[]{:S(2)}) collective-permute-start(f32[2,1,2,256]{3,2,0,1:T(2,128)S(1)} %bitcast.111), channel_id=1, source_target_pairs={{0,352},{32,320},{64,288},{96,256},{128,480},{160,448},{192,416},{... | collective-permute-start | bytes 12296 | tf_op jit(solution)/shard_map/ppermute | solution.py:29
  405.1 5.1 %collective-permute-start.11 = (f32[2,1,2,256]{3,2,0,1:T(2,128)S(1)}, f32[2,1,2,256]{3,2,0,1:T(2,128)S(1)}, u32[]{:S(2)}, u32[]{:S(2)}) collective-permute-start(f32[2,1,2,256]{3,2,0,1:T(2,128)S(1)} %bitcast.110), channel_id=1, source_target_pairs={{0,384},{32,416},{64,448},{96,480},{128,256},{160,288},{192,320},{... | collective-permute-start | bytes 12296 | tf_op jit(solution)/shard_map/ppermute | solution.py:29
  410.2 5.5 %collective-permute-start.12 = (f32[2,1,2,256]{3,2,0,1:T(2,128)S(1)}, f32[2,1,2,256]{3,2,0,1:T(2,128)S(1)}, u32[]{:S(2)}, u32[]{:S(2)}) collective-permute-start(f32[2,1,2,256]{3,2,0,1:T(2,128)S(1)} %bitcast.109), channel_id=1, source_target_pairs={{0,416},{32,384},{64,480},{96,448},{128,288},{160,256},{192,352},{... | collective-permute-start | bytes 12296 | tf_op jit(solution)/shard_map/ppermute | solution.py:29
  415.8 5.8 %collective-permute-start.13 = (f32[2,1,2,256]{3,2,0,1:T(2,128)S(1)}, f32[2,1,2,256]{3,2,0,1:T(2,128)S(1)}, u32[]{:S(2)}, u32[]{:S(2)}) collective-permute-start(f32[2,1,2,256]{3,2,0,1:T(2,128)S(1)} %bitcast.108), channel_id=1, source_target_pairs={{0,448},{32,480},{64,384},{96,416},{128,320},{160,352},{192,256},{... | collective-permute-start | bytes 12296 | tf_op jit(solution)/shard_map/ppermute | solution.py:29
  421.6 1.9 collective-permute-start.14
  423.6 4.7 %collective-permute-done.14 = f32[2,1,2,256]{3,2,0,1:T(2,128)S(1)} collective-permute-done((f32[2,1,2,256]{3,2,0,1:T(2,128)S(1)}, f32[2,1,2,256]{3,2,0,1:T(2,128)S(1)}, u32[]{:S(2)}, u32[]{:S(2)}) %collective-permute-start.14) | collective-permute-done | bytes 4128 | tf_op jit(solution)/shard_map/ppermute | solution.py:29
  428.3 0.6 gather_fusion.2
  428.9 0.6 gather_fusion.3
  429.6 0.7 fusion.6
  (54 shorter events, 0.3 us)
Async XLA Ops:
  7.2 68.9 %copy-start = (bf16[1792,896]{1,0:T(8,128)(2,1)S(1)}, bf16[1792,896]{1,0:T(8,128)(2,1)}, u32[]{:S(2)}) copy-start(bf16[1792,896]{1,0:T(8,128)(2,1)} %param.8) | copy-start | bytes 9633796
  7.2 68.9 %all-gather.3.cloned.1.call-start = ((), (), s32[]{:S(2)}) async-start(), calls=%async_computation.2 | async-start | bytes 3784704 | tf_op jit(solution)/shard_map/all_gather | solution.py:45
  7.9 154.2 %reduce-scatter.3.cloned.1.call-start = ((), (), s32[]{:S(2)}) async-start(), calls=%async_computation.3 | async-start | bytes 3899392 | tf_op jit(solution)/shard_map/reduce_scatter | solution.py:49
  83.8 152.0 %all-gather.5.cloned.1.call-start = ((), (), s32[]{:S(2)}) async-start(), calls=%async_computation.4 | async-start | bytes 1949696 | tf_op jit(solution)/shard_map/all_gather | solution.py:51
  163.7 181.3 %reduce-scatter.5.cloned.1.call-start = ((), (), s32[]{:S(2)}) async-start(), calls=%async_computation.5 | async-start | bytes 2162688 | tf_op jit(solution)/shard_map/reduce_scatter | solution.py:54
  243.7 3.4 copy-start.1
  243.7 4.1 copy-start.2
  243.7 4.8 %copy-start.3 = (s32[16]{0:T(128)S(1)}, s32[16]{0:T(128)}, u32[]{:S(2)}) copy-start(s32[16]{0:T(128)} %param.11) | copy-start | bytes 196
  346.6 20.2 %collective-permute-start = (f32[2,1,2,256]{3,2,0,1:T(2,128)S(1)}, f32[2,1,2,256]{3,2,0,1:T(2,128)S(1)}, u32[]{:S(2)}, u32[]{:S(2)}) collective-permute-start(f32[2,1,2,256]{3,2,0,1:T(2,128)S(1)} %bitcast.121), channel_id=1, source_target_pairs={{0,32},{32,0},{64,96},{96,64},{128,160},{160,128},{192,224},{224,1... | collective-permute-start | bytes 12296 | tf_op jit(solution)/shard_map/ppermute | solution.py:29
  350.1 26.4 %collective-permute-start.1 = (f32[2,1,2,256]{3,2,0,1:T(2,128)S(1)}, f32[2,1,2,256]{3,2,0,1:T(2,128)S(1)}, u32[]{:S(2)}, u32[]{:S(2)}) collective-permute-start(f32[2,1,2,256]{3,2,0,1:T(2,128)S(1)} %bitcast.120), channel_id=1, source_target_pairs={{0,64},{32,96},{64,0},{96,32},{128,192},{160,224},{192,128},{224,1... | collective-permute-start | bytes 12296 | tf_op jit(solution)/shard_map/ppermute | solution.py:29
  354.6 23.8 %collective-permute-start.2 = (f32[2,1,2,256]{3,2,0,1:T(2,128)S(1)}, f32[2,1,2,256]{3,2,0,1:T(2,128)S(1)}, u32[]{:S(2)}, u32[]{:S(2)}) collective-permute-start(f32[2,1,2,256]{3,2,0,1:T(2,128)S(1)} %bitcast.119), channel_id=1, source_target_pairs={{0,96},{32,64},{64,32},{96,0},{128,224},{160,192},{192,160},{224,1... | collective-permute-start | bytes 12296 | tf_op jit(solution)/shard_map/ppermute | solution.py:29
  356.8 34.4 %collective-permute-start.3 = (f32[2,1,2,256]{3,2,0,1:T(2,128)S(1)}, f32[2,1,2,256]{3,2,0,1:T(2,128)S(1)}, u32[]{:S(2)}, u32[]{:S(2)}) collective-permute-start(f32[2,1,2,256]{3,2,0,1:T(2,128)S(1)} %bitcast.118), channel_id=1, source_target_pairs={{0,128},{32,160},{64,192},{96,224},{128,0},{160,32},{192,64},{224,... | collective-permute-start | bytes 12296 | tf_op jit(solution)/shard_map/ppermute | solution.py:29
  364.5 28.6 %collective-permute-start.4 = (f32[2,1,2,256]{3,2,0,1:T(2,128)S(1)}, f32[2,1,2,256]{3,2,0,1:T(2,128)S(1)}, u32[]{:S(2)}, u32[]{:S(2)}) collective-permute-start(f32[2,1,2,256]{3,2,0,1:T(2,128)S(1)} %bitcast.117), channel_id=1, source_target_pairs={{0,160},{32,128},{64,224},{96,192},{128,32},{160,0},{192,96},{224,... | collective-permute-start | bytes 12296 | tf_op jit(solution)/shard_map/ppermute | solution.py:29
  366.8 33.0 %collective-permute-start.5 = (f32[2,1,2,256]{3,2,0,1:T(2,128)S(1)}, f32[2,1,2,256]{3,2,0,1:T(2,128)S(1)}, u32[]{:S(2)}, u32[]{:S(2)}) collective-permute-start(f32[2,1,2,256]{3,2,0,1:T(2,128)S(1)} %bitcast.116), channel_id=1, source_target_pairs={{0,192},{32,224},{64,128},{96,160},{128,64},{160,96},{192,0},{224,... | collective-permute-start | bytes 12296 | tf_op jit(solution)/shard_map/ppermute | solution.py:29
  376.5 28.5 %collective-permute-start.6 = (f32[2,1,2,256]{3,2,0,1:T(2,128)S(1)}, f32[2,1,2,256]{3,2,0,1:T(2,128)S(1)}, u32[]{:S(2)}, u32[]{:S(2)}) collective-permute-start(f32[2,1,2,256]{3,2,0,1:T(2,128)S(1)} %bitcast.115), channel_id=1, source_target_pairs={{0,224},{32,192},{64,160},{96,128},{128,96},{160,64},{192,32},{224... | collective-permute-start | bytes 12296 | tf_op jit(solution)/shard_map/ppermute | solution.py:29
  378.5 31.7 %collective-permute-start.7 = (f32[2,1,2,256]{3,2,0,1:T(2,128)S(1)}, f32[2,1,2,256]{3,2,0,1:T(2,128)S(1)}, u32[]{:S(2)}, u32[]{:S(2)}) collective-permute-start(f32[2,1,2,256]{3,2,0,1:T(2,128)S(1)} %bitcast.114), channel_id=1, source_target_pairs={{0,256},{32,288},{64,320},{96,352},{128,384},{160,416},{192,448},{... | collective-permute-start | bytes 12296 | tf_op jit(solution)/shard_map/ppermute | solution.py:29
  391.2 24.6 %collective-permute-start.8 = (f32[2,1,2,256]{3,2,0,1:T(2,128)S(1)}, f32[2,1,2,256]{3,2,0,1:T(2,128)S(1)}, u32[]{:S(2)}, u32[]{:S(2)}) collective-permute-start(f32[2,1,2,256]{3,2,0,1:T(2,128)S(1)} %bitcast.113), channel_id=1, source_target_pairs={{0,288},{32,256},{64,352},{96,320},{128,416},{160,384},{192,480},{... | collective-permute-start | bytes 12296 | tf_op jit(solution)/shard_map/ppermute | solution.py:29
  393.1 28.5 %collective-permute-start.9 = (f32[2,1,2,256]{3,2,0,1:T(2,128)S(1)}, f32[2,1,2,256]{3,2,0,1:T(2,128)S(1)}, u32[]{:S(2)}, u32[]{:S(2)}) collective-permute-start(f32[2,1,2,256]{3,2,0,1:T(2,128)S(1)} %bitcast.112), channel_id=1, source_target_pairs={{0,320},{32,352},{64,256},{96,288},{128,448},{160,480},{192,384},{... | collective-permute-start | bytes 12296 | tf_op jit(solution)/shard_map/ppermute | solution.py:29
  399.8 23.7 %collective-permute-start.10 = (f32[2,1,2,256]{3,2,0,1:T(2,128)S(1)}, f32[2,1,2,256]{3,2,0,1:T(2,128)S(1)}, u32[]{:S(2)}, u32[]{:S(2)}) collective-permute-start(f32[2,1,2,256]{3,2,0,1:T(2,128)S(1)} %bitcast.111), channel_id=1, source_target_pairs={{0,352},{32,320},{64,288},{96,256},{128,480},{160,448},{192,416},{... | collective-permute-start | bytes 12296 | tf_op jit(solution)/shard_map/ppermute | solution.py:29
  405.1 18.5 %collective-permute-start.11 = (f32[2,1,2,256]{3,2,0,1:T(2,128)S(1)}, f32[2,1,2,256]{3,2,0,1:T(2,128)S(1)}, u32[]{:S(2)}, u32[]{:S(2)}) collective-permute-start(f32[2,1,2,256]{3,2,0,1:T(2,128)S(1)} %bitcast.110), channel_id=1, source_target_pairs={{0,384},{32,416},{64,448},{96,480},{128,256},{160,288},{192,320},{... | collective-permute-start | bytes 12296 | tf_op jit(solution)/shard_map/ppermute | solution.py:29
  410.2 13.4 %collective-permute-start.12 = (f32[2,1,2,256]{3,2,0,1:T(2,128)S(1)}, f32[2,1,2,256]{3,2,0,1:T(2,128)S(1)}, u32[]{:S(2)}, u32[]{:S(2)}) collective-permute-start(f32[2,1,2,256]{3,2,0,1:T(2,128)S(1)} %bitcast.109), channel_id=1, source_target_pairs={{0,416},{32,384},{64,480},{96,448},{128,288},{160,256},{192,352},{... | collective-permute-start | bytes 12296 | tf_op jit(solution)/shard_map/ppermute | solution.py:29
  415.8 7.8 %collective-permute-start.13 = (f32[2,1,2,256]{3,2,0,1:T(2,128)S(1)}, f32[2,1,2,256]{3,2,0,1:T(2,128)S(1)}, u32[]{:S(2)}, u32[]{:S(2)}) collective-permute-start(f32[2,1,2,256]{3,2,0,1:T(2,128)S(1)} %bitcast.108), channel_id=1, source_target_pairs={{0,448},{32,480},{64,384},{96,416},{128,320},{160,352},{192,256},{... | collective-permute-start | bytes 12296 | tf_op jit(solution)/shard_map/ppermute | solution.py:29
  421.6 6.7 %collective-permute-start.14 = (f32[2,1,2,256]{3,2,0,1:T(2,128)S(1)}, f32[2,1,2,256]{3,2,0,1:T(2,128)S(1)}, u32[]{:S(2)}, u32[]{:S(2)}) collective-permute-start(f32[2,1,2,256]{3,2,0,1:T(2,128)S(1)} %bitcast.107), channel_id=1, source_target_pairs={{0,480},{32,448},{64,416},{96,384},{128,352},{160,320},{192,288},{... | collective-permute-start | bytes 12296 | tf_op jit(solution)/shard_map/ppermute | solution.py:29
Sparse Core Ops, SparseCore 0:
  11.1 64.8 all-gather.2
  84.0 78.1 reduce-scatter.2
  164.8 71.0 all-gather.4
  246.4 98.6 reduce-scatter.4
